TPU v7x, 32 devices: a whole 2x2x4 slice. The times are simulated.
32 devices in a mesh: groups: 2 (over x), tm: 16 (over z, y, core).
Axes of the slice: x: 2, y: 2, z: 4, core: 2. Of those that a mesh axis runs over, the one named last changes fastest.
Arguments:
- states: bfloat16 [4096, 2, 1024], P('tm', 'groups'), parts along dimension 1, may hold values from -6 to 6
- goals: bfloat16 [4096, 2, 1024], P('tm', 'groups'), parts along dimension 1, may hold values from -6 to 6
- pos_offset: int32 [16, 2, 8], P('tm', 'groups'), parts along dimension 1, may hold values from 0 to 15
- neg_blocks: int32 [16, 2, 16], P('tm', 'groups'), parts along dimension 1, may hold values from 0 to 15
Outputs:
- loss_mean: float32 [2], P('groups'), parts along dimension 0
- grad_states: float32 [4096, 2, 1024], P('tm', 'groups'), parts along dimension 1
- grad_goals: float32 [4096, 2, 1024], P('tm', 'groups'), parts along dimension 1
There are 2 independent parts, one for each index of `groups`. A program takes and returns all parts, laid end to end along the dimension named above; each array names one. Nothing has to cross between parts.
All inputs are finite; a program needn't handle non-finite values.
Results may differ from a plain program's by a relative error of at most 0.012.
Values may be sent and summed in bfloat16 or wider, within the bound.
No kernel may reach another device: no remote copies, remote signals or barrier semaphores. Data moves between devices by JAX's collectives and lax.ppermute only.
A program may use at most 128 MiB of HBM per device.

v0:
```python
import math
import jax
import jax.numpy as jnp
from jax import lax
from jax.sharding import PartitionSpec as P

E = 1024
L = 256


def pair_weights(pos_offset, neg_blocks, row_first, row_count, col_count):
    block_count = row_count // L
    row_blocks = row_first // L + jnp.arange(block_count, dtype=jnp.int32)
    col_times = jnp.arange(col_count, dtype=jnp.int32)
    col_blocks = col_times // L
    targets = row_blocks[:, None, None] + pos_offset
    pos_count = jnp.sum((targets[..., None] == col_blocks).astype(jnp.float32), axis=2)
    neg_count = jnp.sum((neg_blocks[..., None] == col_blocks).astype(jnp.float32), axis=2)
    pos_count = jnp.repeat(jnp.swapaxes(pos_count, 0, 1), L, axis=1)
    neg_count = jnp.repeat(jnp.swapaxes(neg_count, 0, 1), L, axis=1)
    row_times = row_first + jnp.arange(row_count, dtype=jnp.int32)
    later_mask = (col_times[None, :] > row_times[:, None]).astype(jnp.float32)
    return (pos_count * later_mask, neg_count)


def score_terms(anchor_rows, goal_rows, pos_weight, neg_weight):
    inv_root = 1.0 / math.sqrt(E)
    scores = (
        jnp.einsum("qte,kte->tqk", anchor_rows, goal_rows, preferred_element_type=jnp.float32)
        * inv_root
    )
    loss_sum = jnp.sum(pos_weight * jax.nn.softplus(-scores) + neg_weight * jax.nn.softplus(scores))
    slopes = neg_weight * jax.nn.sigmoid(scores) - pos_weight * jax.nn.sigmoid(-scores)
    return (loss_sum, (slopes * inv_root).astype(jnp.bfloat16))


def per_device(states, goals, pos_offset, neg_blocks):
    row_count = states.shape[0]
    traj_count = states.shape[1]
    steps_all = row_count * lax.axis_size("tm")
    row_first = lax.axis_index("tm") * row_count
    goal_piece = lax.all_gather(goals, "tm", axis=0, tiled=True)
    col_count = goal_piece.shape[0]
    pos_weight, neg_weight = pair_weights(pos_offset, neg_blocks, row_first, row_count, col_count)
    loss_sum, coeffs = score_terms(states, goal_piece, pos_weight, neg_weight)
    grad_rows = jnp.einsum("tqk,kte->qte", coeffs, goal_piece, preferred_element_type=jnp.float32)
    loss_sum, coeffs, grad_rows = (loss_sum, coeffs, grad_rows)
    folded = (grad_rows, loss_sum, coeffs)
    grad_states = folded[0]
    loss_sum = folded[1]
    coeff_all = folded[2]
    grad_goals = lax.psum_scatter(
        jnp.einsum("tqk,qte->kte", coeff_all, states, preferred_element_type=jnp.float32).astype(
            jnp.bfloat16
        ),
        "tm",
        scatter_dimension=0,
        tiled=True,
    ).astype(jnp.float32)
    loss_all = lax.psum(loss_sum, "tm")
    loss_mean = (loss_all / (traj_count * steps_all)).reshape(1)
    return (loss_mean, grad_states, grad_goals)


def solution(mesh):
    in_specs = (
        P("tm", "groups", None),
        P("tm", "groups", None),
        P("tm", "groups", None),
        P("tm", "groups", None),
    )
    out_specs = (P("groups"), P("tm", "groups", None), P("tm", "groups", None))
    return jax.shard_map(
        per_device, mesh=mesh, in_specs=in_specs, out_specs=out_specs, check_vma=False
    )
```

profile of v0, /device:TPU:0, one launch (start us, length us, event | category | flops | bytes accessed | tf_op | source)
XLA Modules:
  0.0 219.8 jit_solution(17836653208547374864)
XLA Ops:
  7.2 0.0 copy-start
  7.2 0.0 all-gather.2.cloned.1.call-start
  7.2 0.7 all-gather.2.cloned.1.call-update
  7.9 0.0 reduce-scatter.2.cloned.1.call-start
  8.0 0.7 add_bitcast_fusion
  8.7 0.1 convert_reduce_fusion.1
  8.8 0.8 convert_reduce_fusion
  9.6 77.6 %all-gather.2.cloned.1.call-done = bf16[4096,1,1024]{2,0,1:T(8,128)(2,1)} async-done(((bf16[256,1,1024]{2,0,1:T(8,128)(2,1)}), bf16[4096,1,1024]{2,0,1:T(8,128)(2,1)}) %all-gather.2.cloned.1.call-update) | async-done | bytes 8388624 | tf_op jit(solution)/shard_map/all_gather | solution.py:42
  87.2 0.0 copy-done
  87.2 11.5 %fusion.8 = (f32[]{:T(128)}, f32[256,4096]{1,0:T(8,128)S(1)}) fusion(f32[4096]{0:T(1024)S(1)} %convert_reduce_fusion, f32[4096]{0:T(1024)S(1)} %convert_reduce_fusion.1, s32[256]{0:T(256)S(1)} %iota_add_fusion, bf16[4096,1,1024]{2,0,1:T(8,128)(2,1)} %all-gather.2.cloned.1.call-done, bf16[256,1,1024]{2,0,1:T(8,128)(2,1)S(1)} %copy-done), kind=kOutput, calls=%fused_computation.11 | convolution fusion | flops 2168455168 | bytes 13140996 | tf_op jit(solution)/shard_map/qte,kte->tqk/dot_general | solution.py:29
  98.7 0.0 copy-start.1
  98.7 1.9 copy-done.1
  100.6 6.2 %convert_bitcast_fusion = bf16[4096,1,1024]{2,0,1:T(8,128)(2,1)} fusion(bf16[256,1,1024]{2,0,1:T(8,128)(2,1)S(1)} %copy-done, f32[256,4096]{1,0:T(8,128)S(1)} %get-tuple-element.10, f32[4096]{0:T(1024)S(1)} %convert_reduce_fusion, f32[4096]{0:T(1024)S(1)} %convert_reduce_fusion.1, s32[256]{0:T(256)S(1)} %iota_add_fusion), kind=kOutput, calls=%fused_computation.6 | convolution fusion | flops 2164260864 | bytes 13140992 | tf_op jit(solution)/shard_map/tqk,qte->kte/dot_general | solution.py:53
  106.8 0.0 reduce-scatter.2.cloned.1.call-update
  106.8 32.1 %psum.7 = f32[]{:T(128)} all-reduce(f32[]{:T(128)} %get-tuple-element.9), channel_id=1, replica_groups=mesh['groups'=2,'tm'=16] {'tm'}, use_global_device_ids=true, to_apply=%region_3.4 | all-reduce | flops 1 | bytes 8 | tf_op jit(solution)/shard_map/psum | solution.py:60
  138.9 8.2 %fusion.13 = f32[256,1,1024]{2,0,1:T(8,128)S(1)} fusion(bf16[4096,1,1024]{2,0,1:T(8,128)(2,1)} %all-gather.2.cloned.1.call-done, f32[256,4096]{1,0:T(8,128)} %copy-done.1, f32[4096]{0:T(1024)S(1)} %convert_reduce_fusion, f32[4096]{0:T(1024)S(1)} %convert_reduce_fusion.1, s32[256]{0:T(256)S(1)} %iota_add_fusion), kind=kOutput, calls=%fused_computation.18 | convolution fusion | flops 2160066560 | bytes 13665280 | tf_op jit(solution)/shard_map/tqk,kte->qte/dot_general | solution.py:46
  147.1 2.0 copy.9
  149.8 59.2 %reduce-scatter.2.cloned.1.call-done = bf16[256,1,1024]{2,0,1:T(8,128)(2,1)} async-done(((bf16[4096,1,1024]{2,0,1:T(8,128)(2,1)}), bf16[256,1,1024]{2,0,1:T(8,128)(2,1)}) %reduce-scatter.2.cloned.1.call-update) | async-done | bytes 524304 | tf_op jit(solution)/shard_map/reduce_scatter | solution.py:52
  209.0 2.8 %copy.10 = f32[256,1,1024]{2,1,0:T(1,128)} copy(bf16[256,1,1024]{2,0,1:T(8,128)(2,1)} %reduce-scatter.2.cloned.1.call-done) | data formatting | bytes 1572864
  (2 shorter events, 0.0 us)
Async XLA Ops:
  7.2 80.0 %copy-start = (bf16[256,1,1024]{2,0,1:T(8,128)(2,1)S(1)}, bf16[256,1,1024]{2,0,1:T(8,128)(2,1)}, u32[]{:S(2)}) copy-start(bf16[256,1,1024]{2,0,1:T(8,128)(2,1)} %param.4) | copy-start | bytes 1572868
  7.2 80.0 %all-gather.2.cloned.1.call-start = ((), (), s32[]{:S(2)}) async-start(), calls=%async_computation.1 | async-start | bytes 8912896 | tf_op jit(solution)/shard_map/all_gather | solution.py:42
  7.9 201.1 %reduce-scatter.2.cloned.1.call-start = ((), (), s32[]{:S(2)}) async-start(), calls=%async_computation.2 | async-start | bytes 8912896 | tf_op jit(solution)/shard_map/reduce_scatter | solution.py:52
  98.7 1.9 copy-start.1
Sparse Core Ops, SparseCore 0:
  10.2 77.0 all-gather.1
  107.0 102.0 reduce-scatter.1
where the time goes:
time: 220 us
  waiting for transfers between devices  138 us (63%)
  blocking collectives  32.1 us (15%)
  matrix products  25.9 us (12%)
  between operations  15.9 us (7%)
  local copies, waits for them, and re-layouts  6.8 us (3%)
    all_gather x1, waiting for transfers between devices, per_device(): goal_piece = lax.all_gather(goals, 'tm', axis=0, tiled=True)  77.6 us
    reduce_scatter x1, waiting for transfers between devices, per_device(): lax.psum_scatter(jnp.einsum('tqk,qte->kte', coeff_all, states, preferred_...  59.2 us
    psum x1, blocking collectives, per_device(): loss_all = lax.psum(loss_sum, 'tm')  32.1 us
    dot_general x1, matrix products, score_terms(): jnp.einsum('qte,kte->tqk', anchor_rows, goal_rows, preferred_element_type...  11.5 us
    dot_general x1, matrix products, per_device(): jnp.einsum('tqk,kte->qte', coeffs, goal_piece, preferred_element_type=jnp...  8.22 us
    unnamed x6, local copies, waits for them, and re-layouts  6.8 us
    dot_general x1, matrix products, per_device(): jnp.einsum('tqk,qte->kte', coeff_all, states, preferred_element_type=jnp....  6.2 us
  transfers between devices with their start and end apart: 2, of which 2 were waited for; matrix products, arithmetic and copies ran while one was open for 5% of the time, Pallas kernels for 0%

commit v1 on v0

--- a/solution.py
+++ b/solution.py
@@ -1,3 +1,4 @@
+import functools
 import math
 import jax
 import jax.numpy as jnp
@@ -6,6 +7,26 @@
 
 E = 1024
 L = 256
+
+
+def _try_all_vectors(shard_in, net_axis, ndim_at):
+    dev_count = lax.axis_size(net_axis)
+    by_rank = [(u, (u + 1) % dev_count) for u in range(dev_count)]
+
+    def take_pipes(right_arr):
+        if len(right_arr) == dev_count:
+            return right_arr
+        b_next = lax.ppermute(right_arr[0], net_axis, by_rank)
+        return take_pipes([b_next, *right_arr])
+
+    answer = take_pipes([shard_in])
+    r1 = jnp.concatenate(answer, axis=ndim_at)
+    return jnp.roll(
+        r1, shift=(lax.axis_index(net_axis) + 1) * shard_in.shape[ndim_at], axis=ndim_at
+    )
+
+
+_time_roads = functools.partial(_try_all_vectors, net_axis="tm", ndim_at=0)
 
 
 def pair_weights(pos_offset, neg_blocks, row_first, row_count, col_count):
@@ -39,7 +60,7 @@
     traj_count = states.shape[1]
     steps_all = row_count * lax.axis_size("tm")
     row_first = lax.axis_index("tm") * row_count
-    goal_piece = lax.all_gather(goals, "tm", axis=0, tiled=True)
+    goal_piece = _time_roads(goals)
     col_count = goal_piece.shape[0]
     pos_weight, neg_weight = pair_weights(pos_offset, neg_blocks, row_first, row_count, col_count)
     loss_sum, coeffs = score_terms(states, goal_piece, pos_weight, neg_weight)

time: 220 us -> 330 us (1.50)
  waiting for transfers between devices: 138 us -> 229 us
  local copies, waits for them, and re-layouts: 6.8 us -> 27.5 us
    ppermute x0 -> x15, waiting for transfers between devices: none -> 169 us  [take_pipes(): b_next = lax.ppermute(right_arr[0], net_axis, by_rank)]
    all_gather x1 -> x0, waiting for transfers between devices: 77.6 us -> none  [per_device(): goal_piece = lax.all_gather(goals, 'tm', axis=0, tiled=True)]
    unnamed x6 -> x71, local copies, waits for them, and re-layouts: 6.8 us -> 27.5 us
  transfers between devices with their start and end apart: 2 -> 16, of which waited for: 2 -> 16; matrix products, arithmetic and copies ran while one was open for 5% -> 4% of each run, Pallas kernels for 0% -> 0%
where the time goes in v1:
time: 330 us; the launch traced here: 329 us
  waiting for transfers between devices  229 us (69%)
  blocking collectives  30.1 us (9%)
  local copies, waits for them, and re-layouts  27.5 us (8%)
  matrix products  23.2 us (7%)
  between operations  16.2 us (5%)
    ppermute x15, waiting for transfers between devices, take_pipes(): b_next = lax.ppermute(right_arr[0], net_axis, by_rank)  169 us
    reduce_scatter x1, waiting for transfers between devices, per_device(): lax.psum_scatter(jnp.einsum('tqk,qte->kte', coeff_all, states, preferred_...  60.2 us
    psum x1, blocking collectives, per_device(): loss_all = lax.psum(loss_sum, 'tm')  30.1 us
    unnamed x71, local copies, waits for them, and re-layouts  27.5 us
    dot_general x1, matrix products, score_terms(): jnp.einsum('qte,kte->tqk', anchor_rows, goal_rows, preferred_element_type...  10.9 us
    dot_general x1, matrix products, per_device(): jnp.einsum('tqk,kte->qte', coeffs, goal_piece, preferred_element_type=jnp...  6.71 us
  transfers between devices with their start and end apart: 16, of which 16 were waited for; matrix products, arithmetic and copies ran while one was open for 4% of the time, Pallas kernels for 0%

profile of v1, /device:TPU:0, one launch (start us, length us, event | category | flops | bytes accessed | tf_op | source)
XLA Modules:
  0.0 328.7 jit_solution(14806740512138797146)
XLA Ops:
  7.2 0.0 reduce-scatter.2.cloned.1.call-start
  7.2 0.5 collective-permute-start
  7.8 12.1 %collective-permute-done = bf16[256,1,1024]{2,0,1:T(8,128)(2,1)S(1)} collective-permute-done((bf16[256,1,1024]{2,0,1:T(8,128)(2,1)}, bf16[256,1,1024]{2,0,1:T(8,128)(2,1)S(1)}, u32[]{:S(2)}, u32[]{:S(2)}) %collective-permute-start) | collective-permute-done | bytes 524320 | tf_op jit(solution)/shard_map/ppermute | solution.py:19
  19.8 11.3 %collective-permute-done.1 = bf16[256,1,1024]{2,0,1:T(8,128)(2,1)S(1)} collective-permute-done((bf16[256,1,1024]{2,0,1:T(8,128)(2,1)S(1)}, bf16[256,1,1024]{2,0,1:T(8,128)(2,1)S(1)}, u32[]{:S(2)}, u32[]{:S(2)}) %collective-permute-start.1) | collective-permute-done | bytes 524320 | tf_op jit(solution)/shard_map/ppermute | solution.py:19
  31.1 11.3 %collective-permute-done.2 = bf16[256,1,1024]{2,0,1:T(8,128)(2,1)S(1)} collective-permute-done((bf16[256,1,1024]{2,0,1:T(8,128)(2,1)S(1)}, bf16[256,1,1024]{2,0,1:T(8,128)(2,1)S(1)}, u32[]{:S(2)}, u32[]{:S(2)}) %collective-permute-start.2) | collective-permute-done | bytes 524320 | tf_op jit(solution)/shard_map/ppermute | solution.py:19
  42.5 11.3 %collective-permute-done.3 = bf16[256,1,1024]{2,0,1:T(8,128)(2,1)S(1)} collective-permute-done((bf16[256,1,1024]{2,0,1:T(8,128)(2,1)S(1)}, bf16[256,1,1024]{2,0,1:T(8,128)(2,1)S(1)}, u32[]{:S(2)}, u32[]{:S(2)}) %collective-permute-start.3) | collective-permute-done | bytes 524320 | tf_op jit(solution)/shard_map/ppermute | solution.py:19
  53.8 11.3 %collective-permute-done.4 = bf16[256,1,1024]{2,0,1:T(8,128)(2,1)S(1)} collective-permute-done((bf16[256,1,1024]{2,0,1:T(8,128)(2,1)S(1)}, bf16[256,1,1024]{2,0,1:T(8,128)(2,1)S(1)}, u32[]{:S(2)}, u32[]{:S(2)}) %collective-permute-start.4) | collective-permute-done | bytes 524320 | tf_op jit(solution)/shard_map/ppermute | solution.py:19
  65.1 0.8 copy-done.3
  65.9 11.3 %collective-permute-done.5 = bf16[256,1,1024]{2,0,1:T(8,128)(2,1)S(1)} collective-permute-done((bf16[256,1,1024]{2,0,1:T(8,128)(2,1)S(1)}, bf16[256,1,1024]{2,0,1:T(8,128)(2,1)S(1)}, u32[]{:S(2)}, u32[]{:S(2)}) %collective-permute-start.5) | collective-permute-done | bytes 524320 | tf_op jit(solution)/shard_map/ppermute | solution.py:19
  77.2 0.8 copy-done.5
  78.0 11.3 %collective-permute-done.6 = bf16[256,1,1024]{2,0,1:T(8,128)(2,1)S(1)} collective-permute-done((bf16[256,1,1024]{2,0,1:T(8,128)(2,1)S(1)}, bf16[256,1,1024]{2,0,1:T(8,128)(2,1)S(1)}, u32[]{:S(2)}, u32[]{:S(2)}) %collective-permute-start.6) | collective-permute-done | bytes 524320 | tf_op jit(solution)/shard_map/ppermute | solution.py:19
  89.3 0.8 copy-done.7
  90.1 11.3 %collective-permute-done.7 = bf16[256,1,1024]{2,0,1:T(8,128)(2,1)S(1)} collective-permute-done((bf16[256,1,1024]{2,0,1:T(8,128)(2,1)S(1)}, bf16[256,1,1024]{2,0,1:T(8,128)(2,1)S(1)}, u32[]{:S(2)}, u32[]{:S(2)}) %collective-permute-start.7) | collective-permute-done | bytes 524320 | tf_op jit(solution)/shard_map/ppermute | solution.py:19
  101.4 0.8 copy-done.9
  102.2 11.3 %collective-permute-done.8 = bf16[256,1,1024]{2,0,1:T(8,128)(2,1)S(1)} collective-permute-done((bf16[256,1,1024]{2,0,1:T(8,128)(2,1)S(1)}, bf16[256,1,1024]{2,0,1:T(8,128)(2,1)S(1)}, u32[]{:S(2)}, u32[]{:S(2)}) %collective-permute-start.8) | collective-permute-done | bytes 524320 | tf_op jit(solution)/shard_map/ppermute | solution.py:19
  113.5 0.8 copy-done.11
  114.3 11.3 %collective-permute-done.9 = bf16[256,1,1024]{2,0,1:T(8,128)(2,1)S(1)} collective-permute-done((bf16[256,1,1024]{2,0,1:T(8,128)(2,1)S(1)}, bf16[256,1,1024]{2,0,1:T(8,128)(2,1)S(1)}, u32[]{:S(2)}, u32[]{:S(2)}) %collective-permute-start.9) | collective-permute-done | bytes 524320 | tf_op jit(solution)/shard_map/ppermute | solution.py:19
  125.6 0.8 copy-done.13
  126.4 11.3 %collective-permute-done.10 = bf16[256,1,1024]{2,0,1:T(8,128)(2,1)S(1)} collective-permute-done((bf16[256,1,1024]{2,0,1:T(8,128)(2,1)S(1)}, bf16[256,1,1024]{2,0,1:T(8,128)(2,1)S(1)}, u32[]{:S(2)}, u32[]{:S(2)}) %collective-permute-start.10) | collective-permute-done | bytes 524320 | tf_op jit(solution)/shard_map/ppermute | solution.py:19
  137.7 0.8 copy-done.15
  138.5 11.3 %collective-permute-done.11 = bf16[256,1,1024]{2,0,1:T(8,128)(2,1)S(1)} collective-permute-done((bf16[256,1,1024]{2,0,1:T(8,128)(2,1)S(1)}, bf16[256,1,1024]{2,0,1:T(8,128)(2,1)S(1)}, u32[]{:S(2)}, u32[]{:S(2)}) %collective-permute-start.11) | collective-permute-done | bytes 524320 | tf_op jit(solution)/shard_map/ppermute | solution.py:19
  149.8 0.8 copy-done.17
  150.6 11.4 %collective-permute-done.12 = bf16[256,1,1024]{2,0,1:T(8,128)(2,1)} collective-permute-done((bf16[256,1,1024]{2,0,1:T(8,128)(2,1)S(1)}, bf16[256,1,1024]{2,0,1:T(8,128)(2,1)}, u32[]{:S(2)}, u32[]{:S(2)}) %collective-permute-start.12) | collective-permute-done | bytes 524320 | tf_op jit(solution)/shard_map/ppermute | solution.py:19
  162.0 11.5 %collective-permute-done.13 = bf16[256,1,1024]{2,0,1:T(8,128)(2,1)} collective-permute-done((bf16[256,1,1024]{2,0,1:T(8,128)(2,1)}, bf16[256,1,1024]{2,0,1:T(8,128)(2,1)}, u32[]{:S(2)}, u32[]{:S(2)}) %collective-permute-start.13) | collective-permute-done | bytes 524320 | tf_op jit(solution)/shard_map/ppermute | solution.py:19
  173.6 0.7 add_bitcast_fusion
  174.2 0.1 convert_reduce_fusion.1
  174.4 0.8 convert_reduce_fusion
  175.1 10.0 %collective-permute-done.14 = bf16[256,1,1024]{2,0,1:T(8,128)(2,1)S(1)} collective-permute-done((bf16[256,1,1024]{2,0,1:T(8,128)(2,1)}, bf16[256,1,1024]{2,0,1:T(8,128)(2,1)S(1)}, u32[]{:S(2)}, u32[]{:S(2)}) %collective-permute-start.14) | collective-permute-done | bytes 524320 | tf_op jit(solution)/shard_map/ppermute | solution.py:19
  185.1 1.1 constant_dynamic-update-slice_fusion.30
  186.2 1.1 constant_dynamic-update-slice_fusion.29
  187.3 1.1 constant_dynamic-update-slice_fusion.28
  188.4 1.1 constant_dynamic-update-slice_fusion.27
  189.5 1.1 constant_dynamic-update-slice_fusion.26
  190.5 1.1 constant_dynamic-update-slice_fusion.25
  191.6 1.1 constant_dynamic-update-slice_fusion.24
  192.7 1.1 constant_dynamic-update-slice_fusion.23
  193.8 1.1 constant_dynamic-update-slice_fusion.22
  194.9 1.1 constant_dynamic-update-slice_fusion.21
  196.1 1.1 constant_dynamic-update-slice_fusion.16
  197.2 1.1 constant_dynamic-update-slice_fusion.14
  198.3 1.1 constant_dynamic-update-slice_fusion.13
  200.1 10.9 %fusion.16 = (bf16[256,4096]{0,1:T(8,128)(2,1)S(1)}, f32[]{:T(128)}) fusion(f32[4096]{0:T(1024)S(1)} %convert_reduce_fusion, f32[4096]{0:T(1024)S(1)} %convert_reduce_fusion.1, s32[256]{0:T(256)S(1)} %iota_add_fusion, bf16[256,1,1024]{2,0,1:T(8,128)(2,1)S(1)} %copy-done, bf16[8192,1,1024]{2,0,1:T(8,128)(2,1)S(1)} %constant_dynamic-update-slice_fusion, ...), kind=kOutput, calls=%fused_computation.17 | convolution fusion | flops 2177892352 | bytes 11043848 | tf_op jit(solution)/shard_map/qte,kte->tqk/dot_general | solution.py:50
  211.0 5.6 %convert_bitcast_fusion = bf16[4096,1,1024]{2,0,1:T(8,128)(2,1)} fusion(bf16[256,4096]{0,1:T(8,128)(2,1)S(1)} %get-tuple-element.9, bf16[256,1,1024]{2,0,1:T(8,128)(2,1)S(1)} %copy-done), kind=kOutput, calls=%fused_computation.6 | convolution fusion | flops 2151677952 | bytes 11010048 | tf_op jit(solution)/shard_map/tqk,qte->kte/dot_general | solution.py:74
  216.6 30.1 %psum.7 = f32[]{:T(128)} all-reduce(f32[]{:T(128)} %get-tuple-element.10), channel_id=1, replica_groups=mesh['groups'=2,'tm'=16] {'tm'}, use_global_device_ids=true, to_apply=%region_3.4 | all-reduce | flops 1 | bytes 8 | tf_op jit(solution)/shard_map/psum | solution.py:81
  246.7 6.7 %fusion.18 = f32[256,1,1024]{0,2,1:T(8,128)} fusion(bf16[256,4096]{0,1:T(8,128)(2,1)S(1)} %get-tuple-element.9, bf16[8192,1,1024]{2,0,1:T(8,128)(2,1)} %copy-done.1, s32[]{:T(128)S(6)} %select_n.40), kind=kOutput, calls=%fused_computation.21 | convolution fusion | flops 2147483648 | bytes 11534340 | tf_op jit(solution)/shard_map/tqk,kte->qte/dot_general | solution.py:67
  253.4 3.6 %copy.9 = f32[256,1,1024]{2,1,0:T(1,128)} copy(f32[256,1,1024]{0,2,1:T(8,128)} %fusion.18) | data formatting | bytes 2097152
  257.7 60.2 %reduce-scatter.2.cloned.1.call-done = bf16[256,1,1024]{2,0,1:T(8,128)(2,1)} async-done(((bf16[4096,1,1024]{2,0,1:T(8,128)(2,1)}), bf16[256,1,1024]{2,0,1:T(8,128)(2,1)}) %reduce-scatter.2.cloned.1.call-update) | async-done | bytes 524304 | tf_op jit(solution)/shard_map/reduce_scatter | solution.py:73
  317.9 2.8 copy.10
  (66 shorter events, 0.8 us)
Async XLA Ops:
  7.2 192.9 %copy-start = (bf16[256,1,1024]{2,0,1:T(8,128)(2,1)S(1)}, bf16[256,1,1024]{2,0,1:T(8,128)(2,1)}, u32[]{:S(2)}) copy-start(bf16[256,1,1024]{2,0,1:T(8,128)(2,1)} %param.4) | copy-start | bytes 1572868
  7.2 192.8 %copy-start.2 = (bf16[256,1,1024]{2,0,1:T(8,128)(2,1)S(1)}, bf16[256,1,1024]{2,0,1:T(8,128)(2,1)}, u32[]{:S(2)}) copy-start(bf16[256,1,1024]{2,0,1:T(8,128)(2,1)} %param.5) | copy-start | bytes 1572868
  7.2 310.7 %reduce-scatter.2.cloned.1.call-start = ((), (), s32[]{:S(2)}) async-start(), calls=%async_computation.1 | async-start | bytes 8912896 | tf_op jit(solution)/shard_map/reduce_scatter | solution.py:73
  7.2 12.6 %collective-permute-start = (bf16[256,1,1024]{2,0,1:T(8,128)(2,1)}, bf16[256,1,1024]{2,0,1:T(8,128)(2,1)S(1)}, u32[]{:S(2)}, u32[]{:S(2)}) collective-permute-start(bf16[256,1,1024]{2,0,1:T(8,128)(2,1)} %param.5), channel_id=1, source_target_pairs={{0,1},{1,2},{2,3},{3,4},{4,5},{5,6},{6,7},{7,8},{8,9},{9,10},{10,1... | collective-permute-start | bytes 1572872 | tf_op jit(solution)/shard_map/ppermute | solution.py:19
  19.8 11.3 %collective-permute-start.1 = (bf16[256,1,1024]{2,0,1:T(8,128)(2,1)S(1)}, bf16[256,1,1024]{2,0,1:T(8,128)(2,1)S(1)}, u32[]{:S(2)}, u32[]{:S(2)}) collective-permute-start(bf16[256,1,1024]{2,0,1:T(8,128)(2,1)S(1)} %collective-permute-done), channel_id=1, source_target_pairs={{0,1},{1,2},{2,3},{3,4},{4,5},{5,6},{6,7},{7,8},{8,9},{9,10},{10,1... | collective-permute-start | bytes 1572872 | tf_op jit(solution)/shard_map/ppermute | solution.py:19
  31.1 11.3 %collective-permute-start.2 = (bf16[256,1,1024]{2,0,1:T(8,128)(2,1)S(1)}, bf16[256,1,1024]{2,0,1:T(8,128)(2,1)S(1)}, u32[]{:S(2)}, u32[]{:S(2)}) collective-permute-start(bf16[256,1,1024]{2,0,1:T(8,128)(2,1)S(1)} %collective-permute-done.1), channel_id=1, source_target_pairs={{0,1},{1,2},{2,3},{3,4},{4,5},{5,6},{6,7},{7,8},{8,9},{9,10},{10,1... | collective-permute-start | bytes 1572872 | tf_op jit(solution)/shard_map/ppermute | solution.py:19
  42.4 11.3 %collective-permute-start.3 = (bf16[256,1,1024]{2,0,1:T(8,128)(2,1)S(1)}, bf16[256,1,1024]{2,0,1:T(8,128)(2,1)S(1)}, u32[]{:S(2)}, u32[]{:S(2)}) collective-permute-start(bf16[256,1,1024]{2,0,1:T(8,128)(2,1)S(1)} %collective-permute-done.2), channel_id=1, source_target_pairs={{0,1},{1,2},{2,3},{3,4},{4,5},{5,6},{6,7},{7,8},{8,9},{9,10},{10,1... | collective-permute-start | bytes 1572872 | tf_op jit(solution)/shard_map/ppermute | solution.py:19
  53.8 11.3 %collective-permute-start.4 = (bf16[256,1,1024]{2,0,1:T(8,128)(2,1)S(1)}, bf16[256,1,1024]{2,0,1:T(8,128)(2,1)S(1)}, u32[]{:S(2)}, u32[]{:S(2)}) collective-permute-start(bf16[256,1,1024]{2,0,1:T(8,128)(2,1)S(1)} %collective-permute-done.3), channel_id=1, source_target_pairs={{0,1},{1,2},{2,3},{3,4},{4,5},{5,6},{6,7},{7,8},{8,9},{9,10},{10,1... | collective-permute-start | bytes 1572872 | tf_op jit(solution)/shard_map/ppermute | solution.py:19
  65.1 0.8 copy-start.3
  65.9 11.3 %collective-permute-start.5 = (bf16[256,1,1024]{2,0,1:T(8,128)(2,1)S(1)}, bf16[256,1,1024]{2,0,1:T(8,128)(2,1)S(1)}, u32[]{:S(2)}, u32[]{:S(2)}) collective-permute-start(bf16[256,1,1024]{2,0,1:T(8,128)(2,1)S(1)} %collective-permute-done.4), channel_id=1, source_target_pairs={{0,1},{1,2},{2,3},{3,4},{4,5},{5,6},{6,7},{7,8},{8,9},{9,10},{10,1... | collective-permute-start | bytes 1572872 | tf_op jit(solution)/shard_map/ppermute | solution.py:19
  77.2 0.8 copy-start.5
  78.0 11.3 %collective-permute-start.6 = (bf16[256,1,1024]{2,0,1:T(8,128)(2,1)S(1)}, bf16[256,1,1024]{2,0,1:T(8,128)(2,1)S(1)}, u32[]{:S(2)}, u32[]{:S(2)}) collective-permute-start(bf16[256,1,1024]{2,0,1:T(8,128)(2,1)S(1)} %collective-permute-done.5), channel_id=1, source_target_pairs={{0,1},{1,2},{2,3},{3,4},{4,5},{5,6},{6,7},{7,8},{8,9},{9,10},{10,1... | collective-permute-start | bytes 1572872 | tf_op jit(solution)/shard_map/ppermute | solution.py:19
  89.3 0.8 copy-start.7
  90.1 11.3 %collective-permute-start.7 = (bf16[256,1,1024]{2,0,1:T(8,128)(2,1)S(1)}, bf16[256,1,1024]{2,0,1:T(8,128)(2,1)S(1)}, u32[]{:S(2)}, u32[]{:S(2)}) collective-permute-start(bf16[256,1,1024]{2,0,1:T(8,128)(2,1)S(1)} %collective-permute-done.6), channel_id=1, source_target_pairs={{0,1},{1,2},{2,3},{3,4},{4,5},{5,6},{6,7},{7,8},{8,9},{9,10},{10,1... | collective-permute-start | bytes 1572872 | tf_op jit(solution)/shard_map/ppermute | solution.py:19
  101.4 0.8 copy-start.9
  102.2 11.3 %collective-permute-start.8 = (bf16[256,1,1024]{2,0,1:T(8,128)(2,1)S(1)}, bf16[256,1,1024]{2,0,1:T(8,128)(2,1)S(1)}, u32[]{:S(2)}, u32[]{:S(2)}) collective-permute-start(bf16[256,1,1024]{2,0,1:T(8,128)(2,1)S(1)} %collective-permute-done.7), channel_id=1, source_target_pairs={{0,1},{1,2},{2,3},{3,4},{4,5},{5,6},{6,7},{7,8},{8,9},{9,10},{10,1... | collective-permute-start | bytes 1572872 | tf_op jit(solution)/shard_map/ppermute | solution.py:19
  113.5 0.8 copy-start.11
  114.3 11.3 %collective-permute-start.9 = (bf16[256,1,1024]{2,0,1:T(8,128)(2,1)S(1)}, bf16[256,1,1024]{2,0,1:T(8,128)(2,1)S(1)}, u32[]{:S(2)}, u32[]{:S(2)}) collective-permute-start(bf16[256,1,1024]{2,0,1:T(8,128)(2,1)S(1)} %collective-permute-done.8), channel_id=1, source_target_pairs={{0,1},{1,2},{2,3},{3,4},{4,5},{5,6},{6,7},{7,8},{8,9},{9,10},{10,1... | collective-permute-start | bytes 1572872 | tf_op jit(solution)/shard_map/ppermute | solution.py:19
  125.6 0.8 copy-start.13
  126.4 11.3 %collective-permute-start.10 = (bf16[256,1,1024]{2,0,1:T(8,128)(2,1)S(1)}, bf16[256,1,1024]{2,0,1:T(8,128)(2,1)S(1)}, u32[]{:S(2)}, u32[]{:S(2)}) collective-permute-start(bf16[256,1,1024]{2,0,1:T(8,128)(2,1)S(1)} %collective-permute-done.9), channel_id=1, source_target_pairs={{0,1},{1,2},{2,3},{3,4},{4,5},{5,6},{6,7},{7,8},{8,9},{9,10},{10,1... | collective-permute-start | bytes 1572872 | tf_op jit(solution)/shard_map/ppermute | solution.py:19
  137.7 0.8 copy-start.15
  138.5 11.3 %collective-permute-start.11 = (bf16[256,1,1024]{2,0,1:T(8,128)(2,1)S(1)}, bf16[256,1,1024]{2,0,1:T(8,128)(2,1)S(1)}, u32[]{:S(2)}, u32[]{:S(2)}) collective-permute-start(bf16[256,1,1024]{2,0,1:T(8,128)(2,1)S(1)} %collective-permute-done.10), channel_id=1, source_target_pairs={{0,1},{1,2},{2,3},{3,4},{4,5},{5,6},{6,7},{7,8},{8,9},{9,10},{10,1... | collective-permute-start | bytes 1572872 | tf_op jit(solution)/shard_map/ppermute | solution.py:19
  149.8 0.8 copy-start.17
  150.5 11.4 %collective-permute-start.12 = (bf16[256,1,1024]{2,0,1:T(8,128)(2,1)S(1)}, bf16[256,1,1024]{2,0,1:T(8,128)(2,1)}, u32[]{:S(2)}, u32[]{:S(2)}) collective-permute-start(bf16[256,1,1024]{2,0,1:T(8,128)(2,1)S(1)} %collective-permute-done.11), channel_id=1, source_target_pairs={{0,1},{1,2},{2,3},{3,4},{4,5},{5,6},{6,7},{7,8},{8,9},{9,10},{10,1... | collective-permute-start | bytes 1572872 | tf_op jit(solution)/shard_map/ppermute | solution.py:19
  162.0 11.6 %collective-permute-start.13 = (bf16[256,1,1024]{2,0,1:T(8,128)(2,1)}, bf16[256,1,1024]{2,0,1:T(8,128)(2,1)}, u32[]{:S(2)}, u32[]{:S(2)}) collective-permute-start(bf16[256,1,1024]{2,0,1:T(8,128)(2,1)} %collective-permute-done.12), channel_id=1, source_target_pairs={{0,1},{1,2},{2,3},{3,4},{4,5},{5,6},{6,7},{7,8},{8,9},{9,10},{10,1... | collective-permute-start | bytes 1572872 | tf_op jit(solution)/shard_map/ppermute | solution.py:19
  162.0 37.4 %copy-start.18 = (bf16[256,1,1024]{2,0,1:T(8,128)(2,1)S(1)}, bf16[256,1,1024]{2,0,1:T(8,128)(2,1)}, u32[]{:S(2)}) copy-start(bf16[256,1,1024]{2,0,1:T(8,128)(2,1)} %copy-done.17) | copy-start | bytes 1572868
  162.0 37.5 %copy-start.16 = (bf16[256,1,1024]{2,0,1:T(8,128)(2,1)S(1)}, bf16[256,1,1024]{2,0,1:T(8,128)(2,1)}, u32[]{:S(2)}) copy-start(bf16[256,1,1024]{2,0,1:T(8,128)(2,1)} %copy-done.15) | copy-start | bytes 1572868
  162.0 37.5 %copy-start.14 = (bf16[256,1,1024]{2,0,1:T(8,128)(2,1)S(1)}, bf16[256,1,1024]{2,0,1:T(8,128)(2,1)}, u32[]{:S(2)}) copy-start(bf16[256,1,1024]{2,0,1:T(8,128)(2,1)} %copy-done.13) | copy-start | bytes 1572868
  162.0 37.6 %copy-start.12 = (bf16[256,1,1024]{2,0,1:T(8,128)(2,1)S(1)}, bf16[256,1,1024]{2,0,1:T(8,128)(2,1)}, u32[]{:S(2)}) copy-start(bf16[256,1,1024]{2,0,1:T(8,128)(2,1)} %copy-done.11) | copy-start | bytes 1572868
  162.0 37.6 %copy-start.10 = (bf16[256,1,1024]{2,0,1:T(8,128)(2,1)S(1)}, bf16[256,1,1024]{2,0,1:T(8,128)(2,1)}, u32[]{:S(2)}) copy-start(bf16[256,1,1024]{2,0,1:T(8,128)(2,1)} %copy-done.9) | copy-start | bytes 1572868
  162.0 37.7 %copy-start.8 = (bf16[256,1,1024]{2,0,1:T(8,128)(2,1)S(1)}, bf16[256,1,1024]{2,0,1:T(8,128)(2,1)}, u32[]{:S(2)}) copy-start(bf16[256,1,1024]{2,0,1:T(8,128)(2,1)} %copy-done.7) | copy-start | bytes 1572868
  162.0 37.7 %copy-start.6 = (bf16[256,1,1024]{2,0,1:T(8,128)(2,1)S(1)}, bf16[256,1,1024]{2,0,1:T(8,128)(2,1)}, u32[]{:S(2)}) copy-start(bf16[256,1,1024]{2,0,1:T(8,128)(2,1)} %copy-done.5) | copy-start | bytes 1572868
  162.0 37.8 %copy-start.4 = (bf16[256,1,1024]{2,0,1:T(8,128)(2,1)S(1)}, bf16[256,1,1024]{2,0,1:T(8,128)(2,1)}, u32[]{:S(2)}) copy-start(bf16[256,1,1024]{2,0,1:T(8,128)(2,1)} %copy-done.3) | copy-start | bytes 1572868
  173.6 11.5 %collective-permute-start.14 = (bf16[256,1,1024]{2,0,1:T(8,128)(2,1)}, bf16[256,1,1024]{2,0,1:T(8,128)(2,1)S(1)}, u32[]{:S(2)}, u32[]{:S(2)}) collective-permute-start(bf16[256,1,1024]{2,0,1:T(8,128)(2,1)} %collective-permute-done.13), channel_id=1, source_target_pairs={{0,1},{1,2},{2,3},{3,4},{4,5},{5,6},{6,7},{7,8},{8,9},{9,10},{10,1... | collective-permute-start | bytes 1572872 | tf_op jit(solution)/shard_map/ppermute | solution.py:19
  200.1 10.9 %copy-start.1 = (bf16[8192,1,1024]{2,0,1:T(8,128)(2,1)}, bf16[8192,1,1024]{2,0,1:T(8,128)(2,1)S(1)}, u32[]{:S(2)}) copy-start(bf16[8192,1,1024]{2,0,1:T(8,128)(2,1)S(1)} %constant_dynamic-update-slice_fusion) | copy-start | bytes 50331652
Sparse Core Ops, SparseCore 0:
  216.7 101.1 reduce-scatter.1
